TPU v7x, 32 devices: a whole 2x2x4 slice. The times are simulated.
32 devices in a mesh: groups: 2 (over x), tm: 16 (over z, y, core).
Axes of the slice: x: 2, y: 2, z: 4, core: 2. Of those that a mesh axis runs over, the one named last changes fastest.
Arguments:
- samples: float32 [16384, 2048], P('groups', 'tm'), parts along dimension 0, may hold values from -6 to 6
- test_matrix: float32 [4096, 256], P(('groups', 'tm')), parts along dimension 0, may hold values from -0.125 to 0.125
Outputs:
- basis: float32 [16384, 256], P(('groups', 'tm')), parts along dimension 0
- coordinates: float32 [512, 2048], P('groups', 'tm'), parts along dimension 0
There are 2 independent parts, one for each index of `groups`. A program takes and returns all parts, laid end to end along the dimension named above; each array names one. Nothing has to cross between parts.
All inputs are finite; a program needn't handle non-finite values.
Results may differ from a plain program's by a relative error of at most 0.0003.
Values sent between devices are 32-bit elements; how exact they have to be, the bound alone decides.
No kernel may reach another device: no remote copies, remote signals or barrier semaphores. Data moves between devices by JAX's collectives and lax.ppermute only.
A program may use at most 64 MiB of HBM per device.

v0:
```python
import jax
import jax.numpy as jnp
from jax import lax
from jax.sharding import PartitionSpec as P


def local_gram(rows):
    return jnp.dot(
        rows.T, rows, precision=lax.Precision.HIGHEST, preferred_element_type=jnp.float32
    )


def local(samples, test_matrix):
    highest = lax.Precision.HIGHEST
    channels = samples.shape[0]
    sample_rows = samples
    sketch = lax.psum_scatter(
        jnp.dot(sample_rows, test_matrix, precision=highest, preferred_element_type=jnp.float32),
        "tm",
        scatter_dimension=0,
        tiled=True,
    )
    sample_rows = samples
    projected = jnp.einsum(
        "rk,rs->ks",
        lax.all_gather(sketch, "tm", axis=0, tiled=True),
        sample_rows,
        precision=highest,
    )
    gram_one = lax.psum(local_gram(sketch), "tm")
    factor_one = jnp.linalg.cholesky(gram_one)
    orthonormal = jax.scipy.linalg.solve_triangular(factor_one, sketch.T, lower=True).T
    coordinates = jax.scipy.linalg.solve_triangular(factor_one, projected, lower=True)
    return (orthonormal * float(channels) ** 0.5, coordinates)


def solution(mesh):
    placed = (P("groups", "tm"), P(("groups", "tm"), None))
    return jax.shard_map(
        local,
        mesh=mesh,
        in_specs=placed,
        out_specs=(P(("groups", "tm"), None), P("groups", "tm")),
        check_vma=False,
    )
```

profile of v0, /device:TPU:0, one launch (start us, length us, event | category | flops | bytes accessed | tf_op | source)
XLA Modules:
  0.0 319.4 jit_solution(12343590044157621184)
XLA Ops:
  7.2 0.0 copy-start
  7.2 0.0 reduce-scatter.2.cloned.1.call-start
  7.2 0.8 copy-done
  8.1 10.4 %fusion.14 = f32[8192,256]{1,0:T(8,128)} fusion(f32[8192,128]{1,0:T(8,128)} %param.2, f32[128,256]{1,0:T(8,128)S(1)} %copy-done), kind=kOutput, calls=%fused_computation.36 | convolution fusion | flops 3221225472 | bytes 12713984 | tf_op jit(solution)/shard_map/dot_general | solution.py:18
  18.5 0.0 reduce-scatter.2.cloned.1.call-update
  18.5 0.0 all-reduce.3.cloned.1.call-start
  18.5 106.3 %reduce-scatter.2.cloned.1.call-done = f32[512,256]{1,0:T(8,128)} async-done(((f32[8192,256]{1,0:T(8,128)}), f32[512,256]{1,0:T(8,128)}) %reduce-scatter.2.cloned.1.call-update) | async-done | bytes 524304 | tf_op jit(solution)/shard_map/reduce_scatter | solution.py:17
  124.8 0.0 copy-start.1
  124.8 3.0 fusion.15
  127.8 0.0 all-reduce.3.cloned.1.call-update
  127.8 0.2 all-gather.2.cloned.1.call-start
  128.0 0.5 all-gather.2.cloned.1.call-update
  128.6 89.7 %all-reduce.3.cloned.1.call-done = f32[256,256]{0,1:T(8,128)} async-done(((f32[256,256]{0,1:T(8,128)}), f32[256,256]{0,1:T(8,128)}) %all-reduce.3.cloned.1.call-update) | async-done | bytes 262160 | tf_op jit(solution)/shard_map/psum | solution.py:30
  218.2 1.1 copy.5
  219.3 1.0 fusion.3
  220.3 11.7 %cholesky.50 = f32[128,128]{1,0:T(8,128)S(1)} custom-call(f32[128,128]{1,0:T(8,128)S(1)} %cholesky.118), custom_call_target="Cholesky" | custom-call | tf_op jit(solution)/shard_map/jit(cholesky)/cholesky | solution.py:31
  232.1 9.8 %custom-call.18 = f32[1,128,128]{1,2,0:T(8,128)S(1)} custom-call(f32[1,128,128]{2,1,0:T(8,128)S(1)} %get-tuple-element.25), custom_call_target="InvertDiagBlocksLowerTriangular" | custom-call | tf_op jit(solution)/shard_map/jit(cholesky)/cholesky | solution.py:31
  241.9 0.2 constant_dynamic-update-slice_fusion.1
  242.1 0.3 convolution_subtract_fusion.2
  242.4 11.7 %cholesky.105 = f32[128,128]{1,0:T(8,128)S(1)} custom-call(f32[128,128]{1,0:T(8,128)S(1)} %convolution_subtract_fusion.2), custom_call_target="Cholesky" | custom-call | tf_op jit(solution)/shard_map/jit(cholesky)/cholesky | solution.py:31
  254.1 0.7 compare_reduce_fusion
  256.1 0.1 triangular_solve.72
  256.2 4.1 %while.1 = (s32[]{:T(128)}, f32[256,256]{1,0:T(8,128)S(1)}, s32[2,2]{1,0:T(2,128)S(1)}, f32[2,128,128]{2,1,0:T(8,128)S(1)}, s32[]{:T(128)}) while((s32[]{:T(128)}, f32[256,256]{1,0:T(8,128)S(1)}, s32[2,2]{1,0:T(2,128)S(1)}, f32[2,128,128]{2,1,0:T(8,128)S(1)}, s32[]{:T(128)}) %tuple.28), condition=%wide.while_cond, body=%wide.while_body.sunk | while | flops 2 | bytes 131189 | solution.py:32
  256.4 0.6 fusion.30
  257.0 1.4 bitcast_dynamic-update-slice_fusion.2
  258.4 0.6 fusion.30
  259.0 1.4 bitcast_dynamic-update-slice_fusion.2
  260.4 19.7 %custom-call.19 = f32[2,128,128]{1,2,0:T(8,128)S(1)} custom-call(f32[2,128,128]{2,1,0:T(8,128)S(1)} %get-tuple-element.9), custom_call_target="InvertDiagBlocksLowerTriangular" | custom-call | tf_op jit(solution)/shard_map/jit(_solve_triangular)/triangular_solve | solution.py:32
  280.0 0.0 copy-done.1
  280.1 0.4 fusion.1
  280.5 0.6 convolution_subtract_fusion
  281.1 0.4 fusion.10
  281.5 0.1 fusion
  281.6 1.0 copy.6
  282.6 12.7 %all-gather.2.cloned.1.call-done = f32[8192,256]{1,0:T(8,128)} async-done(((f32[512,256]{1,0:T(8,128)}), f32[8192,256]{1,0:T(8,128)}) %all-gather.2.cloned.1.call-update) | async-done | bytes 8388624 | tf_op jit(solution)/shard_map/all_gather | solution.py:26
  295.2 16.2 %fusion.16 = f32[256,128]{1,0:T(8,128)S(1)} fusion(f32[8192,256]{1,0:T(8,128)} %all-gather.2.cloned.1.call-done, f32[8192,128]{1,0:T(8,128)} %param.2), kind=kOutput, calls=%fused_computation.38 | convolution fusion | flops 3221225472 | bytes 12713984 | tf_op jit(solution)/shard_map/rk,rs->ks/dot_general | solution.py:24
  311.5 0.3 fusion.4
  311.7 0.2 convolution_subtract_fusion.1
  312.0 0.3 fusion.9
  312.2 0.7 pad_maximum_fusion
  (9 shorter events, 0.1 us)
Async XLA Ops:
  7.2 0.9 copy-start
  7.2 117.6 %reduce-scatter.2.cloned.1.call-start = ((), (), s32[]{:S(2)}) async-start(), calls=%async_computation.1 | async-start | bytes 8912896 | tf_op jit(solution)/shard_map/reduce_scatter | solution.py:17
  18.5 199.7 %all-reduce.3.cloned.1.call-start = ((), (), s32[]{:S(2)}) async-start(), calls=%async_computation.2 | async-start | bytes 524288 | tf_op jit(solution)/shard_map/psum | solution.py:30
  124.8 155.2 %copy-start.1 = (f32[512,256]{1,0:T(8,128)S(1)}, f32[512,256]{1,0:T(8,128)}, u32[]{:S(2)}) copy-start(f32[512,256]{1,0:T(8,128)} %reduce-scatter.2.cloned.1.call-done) | copy-start | bytes 1572868
  127.8 167.4 %all-gather.2.cloned.1.call-start = ((), (), s32[]{:S(2)}) async-start(), calls=%async_computation.3 | async-start | bytes 8912896 | tf_op jit(solution)/shard_map/all_gather | solution.py:26
Sparse Core Ops, SparseCore 0:
  18.6 106.1 reduce-scatter.1
  128.8 89.3 all-reduce.2
  220.4 74.7 all-gather.1
where the time goes:
time: 320 us; the launch traced here: 319 us
  waiting for transfers between devices  209 us (65%)
  other arithmetic  55.4 us (17%)
  matrix products  32.2 us (10%)
  between operations  15.2 us (5%)
  local copies, waits for them, and re-layouts  6.96 us (2%)
    reduce_scatter x1, waiting for transfers between devices, local(): lax.psum_scatter(jnp.dot(sample_rows, test_matrix, precision=highest, pre...  106 us
    psum x1, waiting for transfers between devices, local(): gram_one = lax.psum(local_gram(sketch), 'tm')  89.7 us
    another operation x6, other arithmetic, local(): factor_one = jnp.linalg.cholesky(gram_one)  34 us
    another operation x3, other arithmetic, local(): jax.scipy.linalg.solve_triangular(factor_one, sketch.T, lower=True)  19.7 us
    dot_general x1, matrix products, local(): jnp.einsum('rk,rs->ks', lax.all_gather(sketch, 'tm', axis=0, tiled=True),...  16.2 us
    all_gather x1, waiting for transfers between devices, local(): lax.all_gather(sketch, 'tm', axis=0, tiled=True)  12.7 us
    dot_general x1, matrix products, local(): jnp.dot(sample_rows, test_matrix, precision=highest, preferred_element_ty...  10.4 us
  transfers between devices with their start and end apart: 3, of which 3 were waited for; matrix products, arithmetic and copies ran while one was open for 20% of the time, Pallas kernels for 0%

commit v1 on v0

--- a/solution.py
+++ b/solution.py
@@ -27,7 +27,7 @@
         sample_rows,
         precision=highest,
     )
-    gram_one = lax.psum(local_gram(sketch), "tm")
+    gram_one = jnp.sum(lax.all_gather(local_gram(sketch), "tm"), axis=0)
     factor_one = jnp.linalg.cholesky(gram_one)
     orthonormal = jax.scipy.linalg.solve_triangular(factor_one, sketch.T, lower=True).T
     coordinates = jax.scipy.linalg.solve_triangular(factor_one, projected, lower=True)

time: 320 us -> 278 us (0.87)
  waiting for transfers between devices: 209 us -> 167 us
    psum x1 -> x0, waiting for transfers between devices: 89.7 us -> none  [local(): gram_one = lax.psum(local_gram(sketch), 'tm')]
    all_gather x0 -> x1, waiting for transfers between devices: none -> 49.4 us  [local(): gram_one = jnp.sum(lax.all_gather(local_gram(sketch), 'tm'), axis=0)]
  transfers between devices with their start and end apart: 3 -> 3, of which waited for: 3 -> 3; matrix products, arithmetic and copies ran while one was open for 20% -> 23% of each run, Pallas kernels for 0% -> 0%
where the time goes in v1:
time: 278 us
  waiting for transfers between devices  167 us (60%)
  other arithmetic  56.9 us (20%)
  matrix products  32.2 us (12%)
  between operations  15.1 us (5%)
  local copies, waits for them, and re-layouts  5.88 us (2%)
    reduce_scatter x1, waiting for transfers between devices, local(): lax.psum_scatter(jnp.dot(sample_rows, test_matrix, precision=highest, pre...  106 us
    all_gather x1, waiting for transfers between devices, local(): gram_one = jnp.sum(lax.all_gather(local_gram(sketch), 'tm'), axis=0)  49.4 us
    another operation x6, other arithmetic, local(): factor_one = jnp.linalg.cholesky(gram_one)  33.9 us
    another operation x3, other arithmetic, local(): jax.scipy.linalg.solve_triangular(factor_one, sketch.T, lower=True)  19.7 us
    dot_general x1, matrix products, local(): jnp.einsum('rk,rs->ks', lax.all_gather(sketch, 'tm', axis=0, tiled=True),...  16.2 us
    all_gather x1, waiting for transfers between devices, local(): lax.all_gather(sketch, 'tm', axis=0, tiled=True)  10.9 us
    dot_general x1, matrix products, local(): jnp.dot(sample_rows, test_matrix, precision=highest, preferred_element_ty...  10.4 us
  transfers between devices with their start and end apart: 3, of which 3 were waited for; matrix products, arithmetic and copies ran while one was open for 23% of the time, Pallas kernels for 0%

profile of v1, /device:TPU:0, one launch (start us, length us, event | category | flops | bytes accessed | tf_op | source)
XLA Modules:
  0.0 277.8 jit_solution(17123176891854260317)
XLA Ops:
  7.2 0.0 copy-start
  7.2 0.0 reduce-scatter.2.cloned.1.call-start
  7.2 0.8 copy-done
  8.1 10.4 %fusion.14 = f32[8192,256]{1,0:T(8,128)} fusion(f32[8192,128]{1,0:T(8,128)} %param.2, f32[128,256]{1,0:T(8,128)S(1)} %copy-done), kind=kOutput, calls=%fused_computation.36 | convolution fusion | flops 3221225472 | bytes 12713984 | tf_op jit(solution)/shard_map/dot_general | solution.py:18
  18.5 0.0 reduce-scatter.2.cloned.1.call-update
  18.5 0.0 all-gather.6.cloned.1.call-start
  18.5 106.3 %reduce-scatter.2.cloned.1.call-done = f32[512,256]{1,0:T(8,128)} async-done(((f32[8192,256]{1,0:T(8,128)}), f32[512,256]{1,0:T(8,128)}) %reduce-scatter.2.cloned.1.call-update) | async-done | bytes 524304 | tf_op jit(solution)/shard_map/reduce_scatter | solution.py:17
  124.8 2.9 %fusion.15 = f32[256,256]{1,0:T(8,128)} fusion(f32[512,256]{1,0:T(8,128)} %reduce-scatter.2.cloned.1.call-done), kind=kOutput, calls=%fused_computation.37 | convolution fusion | flops 402653184 | bytes 786432 | tf_op jit(solution)/shard_map/dot_general | solution.py:8
  127.7 0.0 all-gather.6.cloned.1.call-update
  127.8 0.2 all-gather.4.cloned.1.call-start
  128.0 0.5 all-gather.4.cloned.1.call-update
  128.5 49.4 %all-gather.6.cloned.1.call-done = f32[4096,256]{1,0:T(8,128)} async-done(((f32[256,256]{1,0:T(8,128)}), f32[4096,256]{1,0:T(8,128)}) %all-gather.6.cloned.1.call-update) | async-done | bytes 4194320 | tf_op jit(solution)/shard_map/all_gather | solution.py:30
  178.0 0.0 copy-start.1
  178.0 2.5 reduce_sum.9
  180.5 0.1 copy.6
  180.7 11.7 %cholesky.50 = f32[128,128]{1,0:T(8,128)S(1)} custom-call(f32[128,128]{1,0:T(8,128)S(1)} %cholesky.118), custom_call_target="Cholesky" | custom-call | tf_op jit(solution)/shard_map/jit(cholesky)/cholesky | solution.py:31
  192.5 9.8 %custom-call.18 = f32[1,128,128]{1,2,0:T(8,128)S(1)} custom-call(f32[1,128,128]{2,1,0:T(8,128)S(1)} %get-tuple-element.27), custom_call_target="InvertDiagBlocksLowerTriangular" | custom-call | tf_op jit(solution)/shard_map/jit(cholesky)/cholesky | solution.py:31
  202.3 0.2 constant_dynamic-update-slice_fusion.1
  202.5 0.3 convolution_subtract_fusion.2
  202.8 11.7 %cholesky.105 = f32[128,128]{1,0:T(8,128)S(1)} custom-call(f32[128,128]{1,0:T(8,128)S(1)} %convolution_subtract_fusion.2), custom_call_target="Cholesky" | custom-call | tf_op jit(solution)/shard_map/jit(cholesky)/cholesky | solution.py:31
  214.5 0.6 compare_reduce_fusion
  216.4 0.1 triangular_solve.72
  216.5 4.0 %while.1 = (s32[]{:T(128)}, f32[256,256]{1,0:T(8,128)S(1)}, s32[2,2]{1,0:T(2,128)S(1)}, f32[2,128,128]{2,1,0:T(8,128)S(1)}, s32[]{:T(128)}) while((s32[]{:T(128)}, f32[256,256]{1,0:T(8,128)S(1)}, s32[2,2]{1,0:T(2,128)S(1)}, f32[2,128,128]{2,1,0:T(8,128)S(1)}, s32[]{:T(128)}) %tuple.29), condition=%wide.while_cond, body=%wide.while_body.sunk | while | flops 2 | bytes 131189 | solution.py:32
  216.7 0.6 fusion.30
  217.2 1.3 bitcast_dynamic-update-slice_fusion.2
  218.6 0.6 fusion.30
  219.2 1.3 bitcast_dynamic-update-slice_fusion.2
  220.5 19.7 %custom-call.19 = f32[2,128,128]{1,2,0:T(8,128)S(1)} custom-call(f32[2,128,128]{2,1,0:T(8,128)S(1)} %get-tuple-element.9), custom_call_target="InvertDiagBlocksLowerTriangular" | custom-call | tf_op jit(solution)/shard_map/jit(_solve_triangular)/triangular_solve | solution.py:32
  240.2 0.0 copy-done.1
  240.2 0.4 fusion.1
  240.6 0.6 convolution_subtract_fusion
  241.2 0.4 fusion.10
  241.6 0.1 fusion
  241.7 1.0 copy.7
  242.7 10.9 %all-gather.4.cloned.1.call-done = f32[8192,256]{1,0:T(8,128)} async-done(((f32[512,256]{1,0:T(8,128)}), f32[8192,256]{1,0:T(8,128)}) %all-gather.4.cloned.1.call-update) | async-done | bytes 8388624 | tf_op jit(solution)/shard_map/all_gather | solution.py:26
  253.6 16.2 %fusion.16 = f32[256,128]{1,0:T(8,128)S(1)} fusion(f32[8192,256]{1,0:T(8,128)} %all-gather.4.cloned.1.call-done, f32[8192,128]{1,0:T(8,128)} %param.2), kind=kOutput, calls=%fused_computation.38 | convolution fusion | flops 3221225472 | bytes 12713984 | tf_op jit(solution)/shard_map/rk,rs->ks/dot_general | solution.py:24
  269.8 0.3 fusion.4
  270.1 0.2 convolution_subtract_fusion.1
  270.3 0.3 fusion.9
  270.6 0.7 pad_maximum_fusion
  (10 shorter events, 0.2 us)
Async XLA Ops:
  7.2 0.9 copy-start
  7.2 117.6 %reduce-scatter.2.cloned.1.call-start = ((), (), s32[]{:S(2)}) async-start(), calls=%async_computation.1 | async-start | bytes 8912896 | tf_op jit(solution)/shard_map/reduce_scatter | solution.py:17
  18.5 159.5 %all-gather.6.cloned.1.call-start = ((), (), s32[]{:S(2)}) async-start(), calls=%async_computation.3 | async-start | bytes 4456448 | tf_op jit(solution)/shard_map/all_gather | solution.py:30
  127.8 125.8 %all-gather.4.cloned.1.call-start = ((), (), s32[]{:S(2)}) async-start(), calls=%async_computation.2 | async-start | bytes 8912896 | tf_op jit(solution)/shard_map/all_gather | solution.py:26
  178.0 62.2 %copy-start.1 = (f32[512,256]{1,0:T(8,128)S(1)}, f32[512,256]{1,0:T(8,128)}, u32[]{:S(2)}) copy-start(f32[512,256]{1,0:T(8,128)} %reduce-scatter.2.cloned.1.call-done) | copy-start | bytes 1572868
Sparse Core Ops, SparseCore 0:
  18.6 106.1 reduce-scatter.1
  127.9 50.0 all-gather.5
  180.1 73.3 all-gather.3
